TPU v7x, 32 devices: a whole 2x2x4 slice. The times are simulated.
32 devices in a mesh: grp: 4 (over y, core), tm: 8 (over z, x).
Axes of the slice: x: 2, y: 2, z: 4, core: 2. Of those that a mesh axis runs over, the one named last changes fastest.
Arguments:
- wave: bfloat16 [4, 327680], P('grp', 'tm'), may hold values from -6 to 6
- assign: int32 [4, 1024], P('grp', 'tm'), may hold values from 0 to 16383
- w_first: bfloat16 [10, 512], replicated, may hold values from -2 to 2
- w_mid: bfloat16 [4, 1536, 512], replicated, may hold values from -0.15625 to 0.15625
- w_tail: bfloat16 [2, 1024, 512], replicated, may hold values from -0.1875 to 0.1875
- w_proj: bfloat16 [512, 768], replicated, may hold values from -0.25 to 0.25
- centroids: float32 [16384, 768], P('tm'), may hold values from -6 to 6
- prior: float32 [16384], P('tm'), may hold values from 1 to 16
Outputs:
- new_centroids: float32 [16384, 768], P('tm')
- new_counts: float32 [16384], P('tm')
- distortion: float32 [4, 1024], P('grp', 'tm')
All inputs are finite; a program needn't handle non-finite values.
Results may differ from a plain program's by a relative error of at most 0.007.
Values may be sent and summed in bfloat16 or wider, within the bound.
A program may use at most 128 MiB of HBM per device.

v0:
```python
import jax
import jax.numpy as jnp
from jax import lax
from jax.sharding import PartitionSpec as P

HALO = 80
EPS = 1e-05


def passed_along(value, axis, steps):
    count = lax.axis_size(axis)
    leading, last = (max(0, -steps), min(count, count - steps))
    return lax.ppermute(value, axis, [(source, source + steps) for source in range(leading, last)])


def norm_rows(accum):
    row_mean = jnp.mean(accum, axis=-1, keepdims=True)
    centred = accum - row_mean
    spread = jnp.mean(centred * centred, axis=-1, keepdims=True)
    return centred * lax.rsqrt(spread + EPS)


def activate(accum):
    return jax.nn.gelu(norm_rows(accum), approximate=False).astype(jnp.bfloat16)


def first_layer(samples, w_first):
    windows = samples.reshape(-1, 5)
    accum = jnp.dot(windows[:-1], w_first[:5], preferred_element_type=jnp.float32)
    accum = accum + jnp.dot(windows[1:], w_first[5:], preferred_element_type=jnp.float32)
    return activate(accum)


def odd_layer(inputs, weight):
    channels = inputs.shape[1]
    out_len = (inputs.shape[0] - 3) // 2 + 1
    paired = jnp.concatenate([inputs, jnp.zeros((1, channels), inputs.dtype)], axis=0).reshape(
        out_len + 1, 2 * channels
    )
    accum = jnp.dot(paired[:out_len], weight[: 2 * channels], preferred_element_type=jnp.float32)
    accum = accum + jnp.dot(
        paired[1:, :channels], weight[2 * channels :], preferred_element_type=jnp.float32
    )
    return activate(accum)


def even_layer(inputs, weight):
    channels = inputs.shape[1]
    paired = inputs.reshape(inputs.shape[0] // 2, 2 * channels)
    return activate(jnp.dot(paired, weight, preferred_element_type=jnp.float32))


def encode(samples, w_first, w_mid, w_tail):
    hidden = first_layer(samples, w_first)
    for layer_num in range(4):
        hidden = odd_layer(hidden, w_mid[layer_num])
    for layer_num in range(2):
        hidden = even_layer(hidden, w_tail[layer_num])
    return hidden


def project(features, w_proj):
    normed = norm_rows(features.astype(jnp.float32)).astype(jnp.bfloat16)
    return jnp.dot(normed, w_proj, preferred_element_type=jnp.float32).astype(jnp.bfloat16)


def local(wave, assign, w_first, w_mid, w_tail, w_proj, centroids, prior):
    samples = wave[0]
    tail_part = passed_along(samples[:HALO], "tm", -1)
    features = encode(jnp.concatenate([samples, tail_part]), w_first, w_mid, w_tail)
    own_labels = assign[0]
    shard_len = centroids.shape[0]
    feat_width = centroids.shape[1]
    first_id = lax.axis_index("tm") * shard_len
    centroid_ids = first_id + jnp.arange(shard_len, dtype=jnp.int32)
    rounded = lax.optimization_barrier(centroids.astype(jnp.bfloat16))
    widened = rounded.astype(jnp.float32)
    centroid_sq = jnp.sum(widened * widened, axis=1)
    frames = project(features, w_proj)
    accumulate_frames = lax.all_gather(frames, "tm", axis=0, tiled=True)
    labels = lax.all_gather(own_labels, "tm", axis=0, tiled=True)
    one_hot = labels[None, :] == centroid_ids[:, None]
    hot_rows = labels[:, None] == centroid_ids[None, :]
    hot_sums = jnp.dot(
        one_hot.astype(jnp.bfloat16), accumulate_frames, preferred_element_type=jnp.float32
    )
    counts = jnp.sum(one_hot.astype(jnp.float32), axis=1)
    products = jnp.einsum(
        "rd,kd->rk", accumulate_frames, rounded, preferred_element_type=jnp.float32
    )
    frame_wide = accumulate_frames.astype(jnp.float32)
    squares = jnp.sum(frame_wide * frame_wide, axis=1)
    is_owner = (labels >= first_id) & (labels < first_id + shard_len)
    picked = jnp.sum(jnp.where(hot_rows, centroid_sq[None, :] - 2.0 * products, 0.0), axis=1)
    own_term = jnp.where(is_owner, squares + picked, 0.0)
    term_sums = lax.psum_scatter(own_term, "tm", scatter_dimension=0, tiled=True)
    distortion = (term_sums / feat_width)[None, :]
    total_sums, total_counts = (
        lax.psum(hot_sums.astype(jnp.bfloat16), "grp").astype(jnp.float32),
        lax.psum(counts.astype(jnp.bfloat16), "grp").astype(jnp.float32),
    )
    new_counts = prior + total_counts
    new_centroids = (prior[:, None] * centroids + total_sums) / new_counts[:, None]
    return (new_centroids, new_counts, distortion)


def solution(mesh):
    return jax.shard_map(
        local,
        mesh=mesh,
        in_specs=(P("grp", "tm"), P("grp", "tm"), P(), P(), P(), P(), P("tm", None), P("tm")),
        out_specs=(P("tm", None), P("tm"), P("grp", "tm")),
        check_vma=False,
    )
```

profile of v0, /device:TPU:0, one launch (start us, length us, event | category | flops | bytes accessed | tf_op | source)
XLA Modules:
  0.0 410.5 jit_solution(17534476603627418723)
XLA Ops:
  10.6 3.7 collective-permute-done
  14.4 4.5 %slice.152 = bf16[8207,5]{1,0:T(8,128)(2,1)S(1)} reshape(bf16[41035]{0:T(1024)(128)(2,1)S(1)} %get-tuple-element.8) | data formatting | bytes 164140 | tf_op jit(solution)/shard_map/slice | solution.py:30
  19.0 5.9 %slice.149 = bf16[8207,5]{1,0:T(8,128)(2,1)} reshape(bf16[41035]{0:T(1024)(128)(2,1)S(1)} %get-tuple-element.7) | data formatting | bytes 164140 | tf_op jit(solution)/shard_map/slice | solution.py:29
  24.8 8.0 %fusion.115 = f32[8207,512]{1,0:T(8,128)} fusion(bf16[8207,5]{1,0:T(8,128)(2,1)S(1)} %slice.152, bf16[10,512]{1,0:T(8,128)(2,1)S(1)} %copy-done.9), kind=kOutput, calls=%fused_computation.204 | convolution fusion | flops 42019840 | bytes 18917376 | tf_op jit(solution)/shard_map/dot_general | solution.py:30
  32.9 10.8 %fusion.121 = (f32[8207]{0:T(1024)S(1)}, f32[8207,512]{1,0:T(8,128)}) fusion(f32[8207,512]{1,0:T(8,128)} %fusion.115, bf16[8207,5]{1,0:T(8,128)(2,1)S(1)} %copy-done.5, bf16[10,512]{1,0:T(8,128)(2,1)S(1)} %copy-done.9), kind=kOutput, calls=%fused_computation.223 | convolution fusion | flops 50415600 | bytes 35758140 | tf_op jit(solution)/shard_map/dot_general | solution.py:29
  43.7 10.4 %multiply_reduce_fusion = f32[8207]{0:T(1024)S(1)} fusion(f32[8207,512]{1,0:T(8,128)} %get-tuple-element.10, f32[8207]{0:T(1024)S(1)} %broadcast_multiply_fusion), kind=kLoop, calls=%fused_computation.17 | loop fusion | flops 12597745 | bytes 16873592 | tf_op jit(solution)/shard_map/reduce_sum | solution.py:19
  54.4 45.7 %fusion.2 = bf16[8207,512]{1,0:T(8,128)(2,1)} fusion(f32[8207,512]{1,0:T(8,128)S(1)} %copy-done.1, f32[8207]{0:T(1024)S(1)} %add_rsqrt_fusion, f32[8207]{0:T(1024)S(1)} %broadcast_multiply_fusion), kind=kLoop, calls=%fused_computation.3 | loop fusion | flops 281532928 | bytes 25277560 | tf_op jit(solution)/shard_map/convert_element_type | solution.py:24
  100.1 13.0 %slice.155 = bf16[4103,1024]{1,0:T(8,128)(2,1)} reshape(bf16[8206,512]{1,0:T(8,128)(2,1)} %bitcast.63) | data formatting | bytes 16805888 | tf_op jit(solution)/shard_map/slice | solution.py:40
  113.1 8.0 %concatenate.16 = bf16[8208,512]{1,0:T(8,128)(2,1)} pad(bf16[8207,512]{1,0:T(8,128)(2,1)} %fusion.2, bf16[]{:T(256)} %constant.70.clone.1), padding=0_1x0_0 | pad | bytes 16808962 | tf_op jit(solution)/shard_map/concatenate | solution.py:37
  121.1 13.0 %reshape.165 = bf16[4104,1024]{1,0:T(8,128)(2,1)} reshape(bf16[8208,512]{1,0:T(8,128)(2,1)} %concatenate.16) | data formatting | bytes 16809984 | tf_op jit(solution)/shard_map/reshape | solution.py:37
  134.1 7.4 %fusion.64 = f32[4103,512]{1,0:T(8,128)S(1)} fusion(bf16[4103,1024]{1,0:T(8,128)(2,1)} %slice.155, bf16[4,1536,512]{2,1,0:T(8,128)(2,1)} %param.11), kind=kOutput, calls=%fused_computation.114 | convolution fusion | flops 4302307328 | bytes 17856512 | tf_op jit(solution)/shard_map/dot_general | solution.py:40
  141.6 3.7 fusion.122
  147.0 22.3 %fusion.14 = bf16[4103,512]{1,0:T(8,128)(2,1)S(1)} fusion(f32[4103,512]{1,0:T(8,128)S(1)} %get-tuple-element.12, f32[4103]{0:T(1024)S(1)} %add_rsqrt_fusion.1, f32[4103]{0:T(1024)S(1)} %broadcast_multiply_fusion.1), kind=kLoop, calls=%fused_computation.27 | loop fusion | flops 140749312 | bytes 12637240 | tf_op jit(solution)/shard_map/convert_element_type | solution.py:24
  171.3 2.2 concatenate.17
  173.6 7.2 %slice.162 = bf16[2051,1024]{1,0:T(8,128)(2,1)} reshape(bf16[4102,512]{1,0:T(8,128)(2,1)} %bitcast.64) | data formatting | bytes 8400896 | tf_op jit(solution)/shard_map/slice | solution.py:40
  180.7 6.8 %fusion.62 = f32[2051,512]{1,0:T(8,128)} fusion(bf16[2051,1024]{1,0:T(8,128)(2,1)} %slice.162, bf16[4,1536,512]{2,1,0:T(8,128)(2,1)} %param.11), kind=kOutput, calls=%fused_computation.112 | convolution fusion | flops 2150629376 | bytes 9459712 | tf_op jit(solution)/shard_map/dot_general | solution.py:40
  187.5 7.2 %reshape.166 = bf16[2052,1024]{1,0:T(8,128)(2,1)} reshape(bf16[4104,512]{1,0:T(8,128)(2,1)} %concatenate.17) | data formatting | bytes 8404992 | tf_op jit(solution)/shard_map/reshape | solution.py:37
  194.7 4.5 %fusion.123 = (f32[2051]{0:T(1024)S(1)}, f32[2051,512]{1,0:T(8,128)S(1)}) fusion(f32[2051,512]{1,0:T(8,128)} %fusion.62, bf16[4,1536,512]{2,1,0:T(8,128)(2,1)} %param.11, bf16[2052,1024]{1,0:T(8,128)(2,1)} %reshape.166), kind=kOutput, calls=%fused_computation.225 | convolution fusion | flops 1077412864 | bytes 11048972 | tf_op jit(solution)/shard_map/dot_general | solution.py:41
  200.1 11.7 %fusion.25 = bf16[2051,512]{1,0:T(8,128)(2,1)S(1)} fusion(f32[2051,512]{1,0:T(8,128)S(1)} %get-tuple-element.14, f32[2051]{0:T(1024)S(1)} %add_rsqrt_fusion.2, f32[2051]{0:T(1024)S(1)} %broadcast_multiply_fusion.2), kind=kLoop, calls=%fused_computation.53 | loop fusion | flops 70357504 | bytes 6317080 | tf_op jit(solution)/shard_map/convert_element_type | solution.py:24
  215.3 4.6 %fusion.60 = f32[1025,512]{1,0:T(8,128)} fusion(bf16[1025,1024]{1,0:T(8,128)(2,1)} %slice.169, bf16[4,1536,512]{2,1,0:T(8,128)(2,1)} %param.11), kind=kOutput, calls=%fused_computation.110 | convolution fusion | flops 1074790400 | bytes 5261312 | tf_op jit(solution)/shard_map/dot_general | solution.py:40
  221.9 2.9 fusion.124
  225.3 5.7 %fusion.41 = bf16[1025,512]{1,0:T(8,128)(2,1)S(1)} fusion(f32[1025,512]{1,0:T(8,128)S(1)} %get-tuple-element.16, f32[1025]{0:T(1024)S(1)} %add_rsqrt_fusion.3, f32[1025]{0:T(1024)S(1)} %broadcast_multiply_fusion.3), kind=kLoop, calls=%fused_computation.79 | loop fusion | flops 35161600 | bytes 3157000 | tf_op jit(solution)/shard_map/convert_element_type | solution.py:24
  232.3 3.3 fusion.58
  238.0 2.6 fusion.53
  248.3 19.6 %all-gather = s32[1,1024]{1,0:T(1,128)S(1)} all-gather(s32[1,128]{1,0:T(1,128)S(1)} %copy-done.10), channel_id=2, replica_groups=mesh['grp'=4,'tm'=8] {'tm'}, dimensions={1}, use_global_device_ids=true | all-gather | bytes 4608 | tf_op jit(solution)/shard_map/all_gather | solution.py:81
  267.9 26.3 %all-gather.3.cloned.1.call-done = bf16[1024,768]{1,0:T(8,128)(2,1)} async-done(((bf16[128,768]{1,0:T(8,128)(2,1)}), bf16[1024,768]{1,0:T(8,128)(2,1)}) %all-gather.3.cloned.1.call-update) | async-done | bytes 1572880 | tf_op jit(solution)/shard_map/all_gather | solution.py:80
  294.2 6.3 %fusion.36 = bf16[2048,768]{1,0:T(8,128)(2,1)} fusion(bf16[1024,768]{1,0:T(8,128)(2,1)} %all-gather.3.cloned.1.call-done, s32[1024]{0:T(1024)S(1)} %bitcast.66, s32[2048]{0:T(1024)S(1)} %iota_add_fusion), kind=kOutput, calls=%fused_computation.74 | convolution fusion | flops 3224895488 | bytes 4730880 | tf_op jit(solution)/shard_map/dot_general | solution.py:84
  303.0 6.4 %psum.15 = bf16[2048]{0:T(1024)(128)(2,1)S(1)} all-reduce(bf16[2048]{0:T(1024)(128)(2,1)S(1)} %fusion.22), channel_id=1, replica_groups=mesh['grp'=4,'tm'=8] {'grp'}, use_global_device_ids=true, to_apply=%region_18.0 | all-reduce | flops 2048 | bytes 8192 | tf_op jit(solution)/shard_map/psum | solution.py:100
  309.8 58.2 %all-reduce.7.cloned.1.call-done = bf16[2048,768]{1,0:T(8,128)(2,1)} async-done(((bf16[2048,768]{1,0:T(8,128)(2,1)}), bf16[2048,768]{1,0:T(8,128)(2,1)}) %all-reduce.7.cloned.1.call-update) | async-done | bytes 3145744 | tf_op jit(solution)/shard_map/psum | solution.py:99
  368.1 8.7 %fusion.120 = (bf16[2048,768]{1,0:T(8,128)(2,1)S(1)}, f32[2048,768]{1,0:T(8,128)}) fusion(f32[2048,768]{1,0:T(8,128)} %param.14, f32[2048]{0:T(1024)S(1)} %convert_add_fusion, bf16[2048,768]{1,0:T(8,128)(2,1)} %all-reduce.7.cloned.1.call-done, f32[2048]{0:T(1024)S(1)} %copy-done.7), kind=kLoop, calls=%fused_computation.222 | loop fusion | flops 7864320 | bytes 18890752 | tf_op jit(solution)/shard_map/convert_element_type | solution.py:76
  377.4 4.0 select_reduce_fusion
  381.5 21.4 %all-reduce.4 = f32[1024]{0:T(1024)S(1)} all-reduce(f32[1024]{0:T(1024)S(1)} %add_select_fusion), channel_id=3, replica_groups=mesh['grp'=4,'tm'=8] {'tm'}, use_global_device_ids=true, to_apply=%region_22.23.clone | all-reduce | flops 1024 | bytes 8192
  (79 shorter events, 29.0 us)
Async XLA Ops:
  7.2 240.1 %copy-start = (bf16[512,768]{1,0:T(8,128)(2,1)S(1)}, bf16[512,768]{1,0:T(8,128)(2,1)}, u32[]{:S(2)}) copy-start(bf16[512,768]{1,0:T(8,128)(2,1)} %param.13) | copy-start | bytes 2359300
  7.2 17.6 %copy-start.9 = (bf16[10,512]{1,0:T(8,128)(2,1)S(1)}, bf16[10,512]{1,0:T(8,128)(2,1)}, u32[]{:S(2)}) copy-start(bf16[10,512]{1,0:T(8,128)(2,1)} %param.10) | copy-start | bytes 30724
  7.2 287.0 %all-gather.3.cloned.1.call-start = ((), (), s32[]{:S(2)}) async-start(), calls=%async_computation | async-start | bytes 1769472 | tf_op jit(solution)/shard_map/all_gather | solution.py:80
  8.0 6.3 %collective-permute-start = (bf16[80]{0:T(256)(128)(2,1)S(1)}, bf16[80]{0:T(256)(128)(2,1)S(1)}, u32[]{:S(2)}, u32[]{:S(2)}) collective-permute-start(bf16[80]{0:T(256)(128)(2,1)S(1)} %slice_bitcast_fusion), channel_id=1, source_target_pairs={{1,0},{2,1},{3,2},{4,3},{5,4},{6,5},{7,6},{9,8},{10,9},{11,10},{12... | collective-permute-start | bytes 488 | tf_op jit(solution)/shard_map/ppermute | solution.py:13
  24.8 8.0 %copy-start.5 = (bf16[8207,5]{1,0:T(8,128)(2,1)S(1)}, bf16[8207,5]{1,0:T(8,128)(2,1)}, u32[]{:S(2)}) copy-start(bf16[8207,5]{1,0:T(8,128)(2,1)} %slice.149) | copy-start | bytes 246214
  43.7 10.7 %copy-start.1 = (f32[8207,512]{1,0:T(8,128)S(1)}, f32[8207,512]{1,0:T(8,128)}, u32[]{:S(2)}) copy-start(f32[8207,512]{1,0:T(8,128)} %get-tuple-element.10) | copy-start | bytes 50423812
  134.1 7.4 %copy-start.3 = (bf16[4104,1024]{1,0:T(8,128)(2,1)S(1)}, bf16[4104,1024]{1,0:T(8,128)(2,1)}, u32[]{:S(2)}) copy-start(bf16[4104,1024]{1,0:T(8,128)(2,1)} %reshape.165) | copy-start | bytes 25214980
  169.4 1.9 copy-start.2
  215.3 4.6 %copy-start.4 = (bf16[2052,512]{1,0:T(8,128)(2,1)S(1)}, bf16[2052,512]{1,0:T(8,128)(2,1)}, u32[]{:S(2)}) copy-start(bf16[2052,512]{1,0:T(8,128)(2,1)} %concatenate.18) | copy-start | bytes 6303748
  241.0 7.3 %copy-start.10 = (s32[1,128]{1,0:T(1,128)S(1)}, s32[1,128]{1,0:T(1,128)}, u32[]{:S(2)}) copy-start(s32[1,128]{1,0:T(1,128)} %param.9) | copy-start | bytes 1540
  248.3 119.8 %all-reduce.7.cloned.1.call-start = ((), (), s32[]{:S(2)}) async-start(), calls=%async_computation.1 | async-start | bytes 6291456 | tf_op jit(solution)/shard_map/psum | solution.py:99
  294.2 6.4 %copy-start.11 = (u32[32]{0:T(128)S(1)}, u32[32]{0:T(128)}, u32[]{:S(2)}) copy-start(u32[32]{0:T(128)} %constant.30) | copy-start | bytes 388
  294.2 15.2 %copy-start.7 = (f32[2048]{0:T(1024)S(1)}, f32[2048]{0:T(1024)}, u32[]{:S(2)}) copy-start(f32[2048]{0:T(1024)} %param.15) | copy-start | bytes 24580
  300.6 8.8 %copy-start.6 = (bf16[1024,768]{1,0:T(8,128)(2,1)S(1)}, bf16[1024,768]{1,0:T(8,128)(2,1)}, u32[]{:S(2)}) copy-start(bf16[1024,768]{1,0:T(8,128)(2,1)} %all-gather.3.cloned.1.call-done) | copy-start | bytes 4718596
  309.4 67.3 %copy-start.8 = (f32[2048]{0:T(1024)}, f32[2048]{0:T(1024)S(1)}, u32[]{:S(2)}) copy-start(f32[2048]{0:T(1024)S(1)} %convert_add_fusion) | copy-start | bytes 24580
Sparse Core Ops, SparseCore 0:
  248.4 45.8 all-gather.2
  300.7 67.2 all-reduce.6
where the time goes:
time: 418 us; the launch traced here: 410 us
  other arithmetic  117 us (28%)
  waiting for transfers between devices  88.3 us (21%)
  local copies, waits for them, and re-layouts  72.2 us (17%)
  matrix products  68.8 us (16%)
  blocking collectives  47.4 us (11%)
  between operations  15.2 us (4%)
    convert_element_type x6, other arithmetic, activate(): return jax.nn.gelu(norm_rows(accum), approximate=False).astype(jnp.bfloat16)  89.3 us
    psum x1, waiting for transfers between devices, local(): lax.psum(hot_sums.astype(jnp.bfloat16), 'grp').astype(jnp.float32)  58.2 us
    all_gather x1, waiting for transfers between devices, local(): accumulate_frames = lax.all_gather(frames, 'tm', axis=0, tiled=True)  26.3 us
    slice x5, local copies, waits for them, and re-layouts, odd_layer(): paired[:out_len]  23.4 us
    reshape x4, local copies, waits for them, and re-layouts, odd_layer(): jnp.concatenate([inputs, jnp.zeros((1, channels), inputs.dtype)], axis=0)  22.5 us
    dot_general x4, matrix products, odd_layer(): jnp.dot(paired[:out_len], weight[:2 * channels], preferred_element_type=j...  22.1 us
    unnamed x1, blocking collectives  21.4 us
    all_gather x1, blocking collectives, local(): labels = lax.all_gather(own_labels, 'tm', axis=0, tiled=True)  19.6 us
  transfers between devices with their start and end apart: 3, of which 3 were waited for; matrix products, arithmetic and copies ran while one was open for 1% of the time, Pallas kernels for 0%

commit v1 on v0

--- a/solution.py
+++ b/solution.py
@@ -77,7 +77,16 @@
     widened = rounded.astype(jnp.float32)
     centroid_sq = jnp.sum(widened * widened, axis=1)
     frames = project(features, w_proj)
-    accumulate_frames = lax.all_gather(frames, "tm", axis=0, tiled=True)
+    aux, t1 = (lax.axis_size("tm"), lax.axis_index("tm"))
+    accumulate_frames, built = (frames, 1)
+    while built < aux:
+        r_now = lax.ppermute(
+            accumulate_frames, axis_name="tm", perm=tuple(((it, it ^ built) for it in range(aux)))
+        )
+        oldest = jnp.concatenate([accumulate_frames, r_now], axis=0)
+        h_now = jnp.concatenate([r_now, accumulate_frames], axis=0)
+        accumulate_frames = jnp.where(t1 & built == 0, oldest, h_now)
+        built = 2 * built
     labels = lax.all_gather(own_labels, "tm", axis=0, tiled=True)
     one_hot = labels[None, :] == centroid_ids[:, None]
     hot_rows = labels[:, None] == centroid_ids[None, :]

time: 418 us -> 432 us (1.033)
  blocking collectives: 47.4 us -> 55.7 us
  starting transfers between devices: 1.36 us -> 8.5 us
    all_gather x1 -> x0, waiting for transfers between devices: 26.3 us -> none  [local(): accumulate_frames = lax.all_gather(frames, 'tm', axis=0, tiled=True)]
    ppermute x0 -> x3, waiting for transfers between devices: none -> 14.5 us  [local(): lax.ppermute(accumulate_frames, axis_name='tm', perm=tuple(((it, it ^ bui...]
    psum x1, waiting for transfers between devices: 58.2 us -> 68.5 us  [local(): lax.psum(hot_sums.astype(jnp.bfloat16), 'grp').astype(jnp.float32)]
    all_gather x1, blocking collectives: 19.6 us -> 28.6 us  [local(): labels = lax.all_gather(own_labels, 'tm', axis=0, tiled=True)]
    ppermute x0 -> x3, starting transfers between devices: none -> 7.18 us  [local(): lax.ppermute(accumulate_frames, axis_name='tm', perm=tuple(((it, it ^ bui...]
  transfers between devices with their start and end apart: 3 -> 5, of which waited for: 3 -> 5; matrix products, arithmetic and copies ran while one was open for 1% -> 1% of each run, Pallas kernels for 0% -> 0%
where the time goes in v1:
time: 432 us; the launch traced here: 425 us
  other arithmetic  118 us (27%)
  waiting for transfers between devices  86.7 us (20%)
  local copies, waits for them, and re-layouts  72.2 us (17%)
  matrix products  68.4 us (16%)
  blocking collectives  55.7 us (13%)
  between operations  15.3 us (4%)
  starting transfers between devices  8.5 us (2%)
    convert_element_type x6, other arithmetic, activate(): return jax.nn.gelu(norm_rows(accum), approximate=False).astype(jnp.bfloat16)  89.3 us
    psum x1, waiting for transfers between devices, local(): lax.psum(hot_sums.astype(jnp.bfloat16), 'grp').astype(jnp.float32)  68.5 us
    all_gather x1, blocking collectives, local(): labels = lax.all_gather(own_labels, 'tm', axis=0, tiled=True)  28.6 us
    slice x5, local copies, waits for them, and re-layouts, odd_layer(): paired[:out_len]  23.4 us
    reshape x4, local copies, waits for them, and re-layouts, odd_layer(): jnp.concatenate([inputs, jnp.zeros((1, channels), inputs.dtype)], axis=0)  22.5 us
    dot_general x4, matrix products, odd_layer(): jnp.dot(paired[:out_len], weight[:2 * channels], preferred_element_type=j...  22.1 us
    unnamed x1, blocking collectives  21.4 us
    ppermute x3, waiting for transfers between devices, local(): lax.ppermute(accumulate_frames, axis_name='tm', perm=tuple(((it, it ^ bui...  14.5 us
  transfers between devices with their start and end apart: 5, of which 5 were waited for; matrix products, arithmetic and copies ran while one was open for 1% of the time, Pallas kernels for 0%

profile of v1, /device:TPU:0, one launch (start us, length us, event | category | flops | bytes accessed | tf_op | source)
XLA Modules:
  0.0 424.7 jit_solution(16789756094517130445)
XLA Ops:
  10.6 3.7 collective-permute-done
  14.4 4.5 %slice.152 = bf16[8207,5]{1,0:T(8,128)(2,1)S(1)} reshape(bf16[41035]{0:T(1024)(128)(2,1)S(1)} %get-tuple-element.8) | data formatting | bytes 164140 | tf_op jit(solution)/shard_map/slice | solution.py:30
  19.0 5.9 %slice.149 = bf16[8207,5]{1,0:T(8,128)(2,1)} reshape(bf16[41035]{0:T(1024)(128)(2,1)S(1)} %get-tuple-element.7) | data formatting | bytes 164140 | tf_op jit(solution)/shard_map/slice | solution.py:29
  24.8 8.0 %fusion.115 = f32[8207,512]{1,0:T(8,128)} fusion(bf16[8207,5]{1,0:T(8,128)(2,1)S(1)} %slice.152, bf16[10,512]{1,0:T(8,128)(2,1)S(1)} %copy-done.8), kind=kOutput, calls=%fused_computation.207 | convolution fusion | flops 42019840 | bytes 18917376 | tf_op jit(solution)/shard_map/dot_general | solution.py:30
  32.9 10.8 %fusion.121 = (f32[8207]{0:T(1024)S(1)}, f32[8207,512]{1,0:T(8,128)}) fusion(f32[8207,512]{1,0:T(8,128)} %fusion.115, bf16[8207,5]{1,0:T(8,128)(2,1)S(1)} %copy-done.5, bf16[10,512]{1,0:T(8,128)(2,1)S(1)} %copy-done.8), kind=kOutput, calls=%fused_computation.226 | convolution fusion | flops 50415600 | bytes 35758140 | tf_op jit(solution)/shard_map/dot_general | solution.py:29
  43.7 10.4 %multiply_reduce_fusion = f32[8207]{0:T(1024)S(1)} fusion(f32[8207,512]{1,0:T(8,128)} %get-tuple-element.10, f32[8207]{0:T(1024)S(1)} %broadcast_multiply_fusion), kind=kLoop, calls=%fused_computation.17 | loop fusion | flops 12597745 | bytes 16873592 | tf_op jit(solution)/shard_map/reduce_sum | solution.py:19
  54.4 45.7 %fusion.2 = bf16[8207,512]{1,0:T(8,128)(2,1)} fusion(f32[8207,512]{1,0:T(8,128)S(1)} %copy-done.1, f32[8207]{0:T(1024)S(1)} %add_rsqrt_fusion, f32[8207]{0:T(1024)S(1)} %broadcast_multiply_fusion), kind=kLoop, calls=%fused_computation.3 | loop fusion | flops 281532928 | bytes 25277560 | tf_op jit(solution)/shard_map/convert_element_type | solution.py:24
  100.0 13.0 %slice.155 = bf16[4103,1024]{1,0:T(8,128)(2,1)} reshape(bf16[8206,512]{1,0:T(8,128)(2,1)} %bitcast.61) | data formatting | bytes 16805888 | tf_op jit(solution)/shard_map/slice | solution.py:40
  113.1 8.0 %concatenate.34 = bf16[8208,512]{1,0:T(8,128)(2,1)} pad(bf16[8207,512]{1,0:T(8,128)(2,1)} %fusion.2, bf16[]{:T(256)} %constant.78.clone.1), padding=0_1x0_0 | pad | bytes 16808962 | tf_op jit(solution)/shard_map/concatenate | solution.py:37
  121.1 13.0 %reshape.165 = bf16[4104,1024]{1,0:T(8,128)(2,1)} reshape(bf16[8208,512]{1,0:T(8,128)(2,1)} %concatenate.34) | data formatting | bytes 16809984 | tf_op jit(solution)/shard_map/reshape | solution.py:37
  134.1 7.4 %fusion.64 = f32[4103,512]{1,0:T(8,128)S(1)} fusion(bf16[4103,1024]{1,0:T(8,128)(2,1)} %slice.155, bf16[4,1536,512]{2,1,0:T(8,128)(2,1)} %param.11), kind=kOutput, calls=%fused_computation.115 | convolution fusion | flops 4302307328 | bytes 17856512 | tf_op jit(solution)/shard_map/dot_general | solution.py:40
  141.5 3.8 fusion.122
  147.0 22.3 %fusion.14 = bf16[4103,512]{1,0:T(8,128)(2,1)S(1)} fusion(f32[4103,512]{1,0:T(8,128)S(1)} %get-tuple-element.12, f32[4103]{0:T(1024)S(1)} %add_rsqrt_fusion.1, f32[4103]{0:T(1024)S(1)} %broadcast_multiply_fusion.1), kind=kLoop, calls=%fused_computation.27 | loop fusion | flops 140749312 | bytes 12637240 | tf_op jit(solution)/shard_map/convert_element_type | solution.py:24
  173.5 7.2 %slice.162 = bf16[2051,1024]{1,0:T(8,128)(2,1)} reshape(bf16[4102,512]{1,0:T(8,128)(2,1)} %bitcast.62) | data formatting | bytes 8400896 | tf_op jit(solution)/shard_map/slice | solution.py:40
  180.7 6.8 %fusion.62 = f32[2051,512]{1,0:T(8,128)} fusion(bf16[2051,1024]{1,0:T(8,128)(2,1)} %slice.162, bf16[4,1536,512]{2,1,0:T(8,128)(2,1)} %param.11), kind=kOutput, calls=%fused_computation.113 | convolution fusion | flops 2150629376 | bytes 9459712 | tf_op jit(solution)/shard_map/dot_general | solution.py:40
  187.5 7.2 %reshape.166 = bf16[2052,1024]{1,0:T(8,128)(2,1)} reshape(bf16[4104,512]{1,0:T(8,128)(2,1)} %concatenate.35) | data formatting | bytes 8404992 | tf_op jit(solution)/shard_map/reshape | solution.py:37
  194.6 4.5 %fusion.123 = (f32[2051]{0:T(1024)S(1)}, f32[2051,512]{1,0:T(8,128)S(1)}) fusion(f32[2051,512]{1,0:T(8,128)} %fusion.62, bf16[4,1536,512]{2,1,0:T(8,128)(2,1)} %param.11, bf16[2052,1024]{1,0:T(8,128)(2,1)} %reshape.166), kind=kOutput, calls=%fused_computation.228 | convolution fusion | flops 1077412864 | bytes 11048972 | tf_op jit(solution)/shard_map/dot_general | solution.py:41
  200.1 11.7 %fusion.25 = bf16[2051,512]{1,0:T(8,128)(2,1)S(1)} fusion(f32[2051,512]{1,0:T(8,128)S(1)} %get-tuple-element.14, f32[2051]{0:T(1024)S(1)} %add_rsqrt_fusion.2, f32[2051]{0:T(1024)S(1)} %broadcast_multiply_fusion.2), kind=kLoop, calls=%fused_computation.53 | loop fusion | flops 70357504 | bytes 6317080 | tf_op jit(solution)/shard_map/convert_element_type | solution.py:24
  215.2 4.6 %fusion.60 = f32[1025,512]{1,0:T(8,128)} fusion(bf16[1025,1024]{1,0:T(8,128)(2,1)} %slice.169, bf16[4,1536,512]{2,1,0:T(8,128)(2,1)} %param.11), kind=kOutput, calls=%fused_computation.111 | convolution fusion | flops 1074790400 | bytes 5261312 | tf_op jit(solution)/shard_map/dot_general | solution.py:40
  225.3 5.7 %fusion.41 = bf16[1025,512]{1,0:T(8,128)(2,1)S(1)} fusion(f32[1025,512]{1,0:T(8,128)S(1)} %get-tuple-element.16, f32[1025]{0:T(1024)S(1)} %add_rsqrt_fusion.3, f32[1025]{0:T(1024)S(1)} %broadcast_multiply_fusion.3), kind=kLoop, calls=%fused_computation.79 | loop fusion | flops 35161600 | bytes 3157000 | tf_op jit(solution)/shard_map/convert_element_type | solution.py:24
  232.3 3.3 fusion.58
  247.5 3.0 collective-permute-start.1
  250.5 3.8 collective-permute-done.1
  256.0 7.5 %collective-permute-done.2 = bf16[256,768]{1,0:T(8,128)(2,1)S(1)} collective-permute-done((bf16[256,768]{1,0:T(8,128)(2,1)S(1)}, bf16[256,768]{1,0:T(8,128)(2,1)S(1)}, u32[]{:S(2)}, u32[]{:S(2)}) %collective-permute-start.2) | collective-permute-done | bytes 393248 | tf_op jit(solution)/shard_map/ppermute | solution.py:83
  266.4 28.6 %all-gather = s32[1,1024]{1,0:T(1,128)S(1)} all-gather(s32[1,128]{1,0:T(1,128)S(1)} %copy-done.9), channel_id=2, replica_groups=mesh['grp'=4,'tm'=8] {'tm'}, dimensions={1}, use_global_device_ids=true | all-gather | bytes 4608 | tf_op jit(solution)/shard_map/all_gather | solution.py:90
  295.1 3.2 collective-permute-done.3
  298.3 5.5 %fusion.36 = bf16[2048,768]{1,0:T(8,128)(2,1)} fusion(s32[1024]{0:T(1024)S(1)} %bitcast.64, s32[2048]{0:T(1024)S(1)} %iota_add_fusion, bf16[512,768]{1,0:T(8,128)(2,1)S(1)} %collective-permute-done.3, bf16[512,768]{1,0:T(8,128)(2,1)S(1)} %maximum_select_fusion.1, pred[]{:T(512)S(6)} %eq.38), kind=kOutput, calls=%fused_computation.74 | convolution fusion | flops 3231973376 | bytes 4730881 | tf_op jit(solution)/shard_map/dot_general | solution.py:93
  306.1 5.7 %psum.15 = bf16[2048]{0:T(1024)(128)(2,1)S(1)} all-reduce(bf16[2048]{0:T(1024)(128)(2,1)S(1)} %fusion.22), channel_id=1, replica_groups=mesh['grp'=4,'tm'=8] {'grp'}, use_global_device_ids=true, to_apply=%region_18.19 | all-reduce | flops 2048 | bytes 8192 | tf_op jit(solution)/shard_map/psum | solution.py:109
  312.4 68.5 %all-reduce.7.cloned.1.call-done = bf16[2048,768]{1,0:T(8,128)(2,1)} async-done(((bf16[2048,768]{1,0:T(8,128)(2,1)}), bf16[2048,768]{1,0:T(8,128)(2,1)}) %all-reduce.7.cloned.1.call-update) | async-done | bytes 3145744 | tf_op jit(solution)/shard_map/psum | solution.py:108
  380.9 8.9 %fusion.120 = (bf16[2048,768]{1,0:T(8,128)(2,1)S(1)}, f32[2048,768]{1,0:T(8,128)}) fusion(f32[2048,768]{1,0:T(8,128)} %param.14, f32[2048]{0:T(1024)S(1)} %convert_add_fusion, bf16[2048,768]{1,0:T(8,128)(2,1)} %all-reduce.7.cloned.1.call-done, f32[2048]{0:T(1024)S(1)} %copy-done.6), kind=kLoop, calls=%fused_computation.225 | loop fusion | flops 7864320 | bytes 18890752 | tf_op jit(solution)/shard_map/convert_element_type | solution.py:76
  390.5 5.2 %select_reduce_fusion = f32[1024]{0:T(1024)S(1)} fusion(bf16[2048,768]{1,0:T(8,128)(2,1)S(1)} %get-tuple-element.5, f32[2048]{0:T(1024)S(1)} %multiply_reduce_fusion.2, s32[2048]{0:T(1024)S(1)} %iota_add_fusion, s32[1024]{0:T(1024)S(1)} %bitcast.66, bf16[512,768]{1,0:T(8,128)(2,1)S(1)} %collective-permute-done.3, ...), kind=kOutput, calls=%fused_computation.45 | convolution fusion | flops 3238788096 | bytes 4743169 | tf_op jit(solution)/shard_map/rd,kd->rk/dot_general | solution.py:97
  395.7 21.4 %all-reduce.4 = f32[1024]{0:T(1024)S(1)} all-reduce(f32[1024]{0:T(1024)S(1)} %add_select_fusion), channel_id=3, replica_groups=mesh['grp'=4,'tm'=8] {'tm'}, use_global_device_ids=true, to_apply=%region_22.23.clone | all-reduce | flops 1024 | bytes 8192
  (82 shorter events, 40.8 us)
Async XLA Ops:
  7.2 240.0 %copy-start = (bf16[512,768]{1,0:T(8,128)(2,1)S(1)}, bf16[512,768]{1,0:T(8,128)(2,1)}, u32[]{:S(2)}) copy-start(bf16[512,768]{1,0:T(8,128)(2,1)} %param.13) | copy-start | bytes 2359300
  7.2 17.6 %copy-start.8 = (bf16[10,512]{1,0:T(8,128)(2,1)S(1)}, bf16[10,512]{1,0:T(8,128)(2,1)}, u32[]{:S(2)}) copy-start(bf16[10,512]{1,0:T(8,128)(2,1)} %param.10) | copy-start | bytes 30724
  7.2 373.7 %all-reduce.7.cloned.1.call-start = ((), (), s32[]{:S(2)}) async-start(), calls=%async_computation | async-start | bytes 6291456 | tf_op jit(solution)/shard_map/psum | solution.py:108
  8.0 6.3 %collective-permute-start = (bf16[80]{0:T(256)(128)(2,1)S(1)}, bf16[80]{0:T(256)(128)(2,1)S(1)}, u32[]{:S(2)}, u32[]{:S(2)}) collective-permute-start(bf16[80]{0:T(256)(128)(2,1)S(1)} %slice_bitcast_fusion), channel_id=1, source_target_pairs={{1,0},{2,1},{3,2},{4,3},{5,4},{6,5},{7,6},{9,8},{10,9},{11,10},{12... | collective-permute-start | bytes 488 | tf_op jit(solution)/shard_map/ppermute | solution.py:13
  24.8 8.0 %copy-start.5 = (bf16[8207,5]{1,0:T(8,128)(2,1)S(1)}, bf16[8207,5]{1,0:T(8,128)(2,1)}, u32[]{:S(2)}) copy-start(bf16[8207,5]{1,0:T(8,128)(2,1)} %slice.149) | copy-start | bytes 246214
  43.7 10.7 %copy-start.1 = (f32[8207,512]{1,0:T(8,128)S(1)}, f32[8207,512]{1,0:T(8,128)}, u32[]{:S(2)}) copy-start(f32[8207,512]{1,0:T(8,128)} %get-tuple-element.10) | copy-start | bytes 50423812
  134.1 7.4 %copy-start.3 = (bf16[4104,1024]{1,0:T(8,128)(2,1)S(1)}, bf16[4104,1024]{1,0:T(8,128)(2,1)}, u32[]{:S(2)}) copy-start(bf16[4104,1024]{1,0:T(8,128)(2,1)} %reshape.165) | copy-start | bytes 25214980
  169.3 1.9 copy-start.2
  215.2 4.6 %copy-start.4 = (bf16[2052,512]{1,0:T(8,128)(2,1)S(1)}, bf16[2052,512]{1,0:T(8,128)(2,1)}, u32[]{:S(2)}) copy-start(bf16[2052,512]{1,0:T(8,128)(2,1)} %concatenate.36) | copy-start | bytes 6303748
  242.7 23.7 %copy-start.9 = (s32[1,128]{1,0:T(1,128)S(1)}, s32[1,128]{1,0:T(1,128)}, u32[]{:S(2)}) copy-start(s32[1,128]{1,0:T(1,128)} %param.9) | copy-start | bytes 1540
  247.5 6.8 %collective-permute-start.1 = (bf16[128,768]{1,0:T(8,128)(2,1)S(1)}, bf16[128,768]{1,0:T(8,128)(2,1)S(1)}, u32[]{:S(2)}, u32[]{:S(2)}) collective-permute-start(bf16[128,768]{1,0:T(8,128)(2,1)S(1)} %convolution_convert_fusion), channel_id=1, source_target_pairs={{0,1},{1,0},{2,3},{3,2},{4,5},{5,4},{6,7},{7,6},{8,9},{9,8},{10,11... | collective-permute-start | bytes 589832 | tf_op jit(solution)/shard_map/ppermute | solution.py:83
  254.4 9.2 %collective-permute-start.2 = (bf16[256,768]{1,0:T(8,128)(2,1)S(1)}, bf16[256,768]{1,0:T(8,128)(2,1)S(1)}, u32[]{:S(2)}, u32[]{:S(2)}) collective-permute-start(bf16[256,768]{1,0:T(8,128)(2,1)S(1)} %maximum_select_fusion.2), channel_id=1, source_target_pairs={{0,2},{1,3},{2,0},{3,1},{4,6},{5,7},{6,4},{7,5},{8,10},{9,11},{10,... | collective-permute-start | bytes 1179656 | tf_op jit(solution)/shard_map/ppermute | solution.py:83
  263.8 34.4 %collective-permute-start.3 = (bf16[512,768]{1,0:T(8,128)(2,1)S(1)}, bf16[512,768]{1,0:T(8,128)(2,1)S(1)}, u32[]{:S(2)}, u32[]{:S(2)}) collective-permute-start(bf16[512,768]{1,0:T(8,128)(2,1)S(1)} %maximum_select_fusion.1), channel_id=1, source_target_pairs={{0,4},{1,5},{2,6},{3,7},{4,0},{5,1},{6,2},{7,3},{8,12},{9,13},{10,... | collective-permute-start | bytes 2359304 | tf_op jit(solution)/shard_map/ppermute | solution.py:83
  298.3 5.5 %copy-start.10 = (u32[32]{0:T(128)S(1)}, u32[32]{0:T(128)}, u32[]{:S(2)}) copy-start(u32[32]{0:T(128)} %constant.30) | copy-start | bytes 388
  298.3 13.5 %copy-start.6 = (f32[2048]{0:T(1024)S(1)}, f32[2048]{0:T(1024)}, u32[]{:S(2)}) copy-start(f32[2048]{0:T(1024)} %param.15) | copy-start | bytes 24580
  311.8 78.0 %copy-start.7 = (f32[2048]{0:T(1024)}, f32[2048]{0:T(1024)S(1)}, u32[]{:S(2)}) copy-start(f32[2048]{0:T(1024)S(1)} %convert_add_fusion) | copy-start | bytes 24580
Sparse Core Ops, SparseCore 0:
  303.9 76.9 all-reduce.6
